TPU v7x, 32 devices: a whole 2x2x4 slice. The times are simulated.
32 devices in a mesh: prec: 16 (over z, x, core), run: 2 (over y).
Axes of the slice: x: 2, y: 2, z: 4, core: 2. Of those that a mesh axis runs over, the one named last changes fastest.
Arguments:
- intensity: bfloat16 [1024, 32768], P('run', 'prec'), may hold values from -6 to 6
- observed: int32 [1024, 4096], P('run', 'prec'), may hold values from 0 to 255, as said below
- run_factors: bfloat16 [1024, 64], P('run'), as said below
- prec_factors: bfloat16 [32768, 64], P('prec'), as said below
Outputs:
- completed: bfloat16 [1024, 32768], P('run', 'prec')
Inputs may be any that keep to these rules, and one draw needn't show every extreme that they name: `observed`: each word packs eight observation flags in its low 8 bits: bit b of word j is the flag of precursor 8 j + b. `run_factors`: rows of the starting factors have scales that vary along the rows. `prec_factors`: rows of the starting factors have scales that vary along the rows.
All inputs are finite; a program needn't handle non-finite values.
Results may differ from a plain program's by a relative error of at most 0.005.
Values may be sent and summed in bfloat16 or wider, within the bound.
A program may use at most 64 MiB of HBM per device.

v0:
```python
import jax
import jax.numpy as jnp
from jax import lax
from jax.sharding import PartitionSpec as P

ITERS = 4
ridge_value = 16.0


def unpack_mask(words):
    shifts = jnp.arange(8, dtype=jnp.int32)
    bits = jnp.right_shift(words[:, :, None], shifts) & 1
    return bits.reshape(words.shape[0], -1).astype(jnp.float32)


def ridge_solve(matrix, gram):
    size = gram.shape[0]
    factor = jnp.linalg.cholesky(gram + ridge_value * jnp.eye(size, dtype=jnp.float32))
    return jax.scipy.linalg.cho_solve((factor, True), matrix.T).T


def inner_gram(factors):
    return lax.dot_general(
        factors, factors, (((0,), (0,)), ((), ())), preferred_element_type=jnp.float32
    )


def masked_resid(intensity, maskf, u_now, v_now):
    fit = jnp.dot(u_now, v_now.T, preferred_element_type=jnp.float32)
    return (maskf * (intensity.astype(jnp.float32) - fit)).astype(jnp.bfloat16)


def local(intensity, observed, run_factors, prec_factors):
    maskf = unpack_mask(observed)
    u_now = run_factors
    v_now = prec_factors
    for step in range(ITERS):
        resid = masked_resid(intensity, maskf, u_now, v_now)
        proj_part = jnp.dot(resid, v_now, preferred_element_type=jnp.float32)
        gram_part = inner_gram(v_now)
        gram_v = lax.psum(gram_part, "prec")
        share = lax.psum_scatter(proj_part, "prec", scatter_dimension=0, tiled=True)
        count = share.shape[0]
        first = lax.axis_index("prec") * count
        mine = lax.dynamic_slice_in_dim(u_now, first, count, 0)
        total = jnp.dot(mine.astype(jnp.float32), gram_v, precision=lax.Precision.HIGHEST) + share
        fresh = ridge_solve(total, gram_v).astype(jnp.bfloat16)
        u_now = lax.all_gather(fresh, "prec", axis=0, tiled=True)
        resid = masked_resid(intensity, maskf, u_now, v_now)
        proj_part = lax.dot_general(
            resid, u_now, (((0,), (0,)), ((), ())), preferred_element_type=jnp.float32
        )
        gram_part = inner_gram(u_now)
        proj_v, gram_u = (
            lax.psum(proj_part.astype(jnp.bfloat16), "run").astype(jnp.float32),
            lax.psum(gram_part.astype(jnp.bfloat16), "run").astype(jnp.float32),
        )
        total = jnp.dot(v_now.astype(jnp.float32), gram_u, precision=lax.Precision.HIGHEST) + proj_v
        v_now = ridge_solve(total, gram_u).astype(jnp.bfloat16)
    fit = jnp.dot(u_now, v_now.T, preferred_element_type=jnp.float32)
    return (maskf * intensity.astype(jnp.float32) + (1.0 - maskf) * fit).astype(jnp.bfloat16)


def solution(mesh):
    return jax.shard_map(
        local,
        mesh=mesh,
        in_specs=(P("run", "prec"), P("run", "prec"), P("run", None), P("prec", None)),
        out_specs=P("run", "prec"),
        check_vma=False,
    )
```

profile of v0, /device:TPU:0, one launch (start us, length us, event | category | flops | bytes accessed | tf_op | source)
XLA Modules:
  0.0 746.3 jit_solution(6776300041927255322)
XLA Ops:
  6.5 1.3 copy.21
  7.8 2.5 broadcast_bitcast_fusion
  10.3 5.5 copy.22
  16.0 4.4 fusion.26
  20.7 63.0 %psum.84 = f32[64,64]{0,1:T(8,128)S(1)} all-reduce(f32[64,64]{0,1:T(8,128)S(1)} %fusion.103), channel_id=1, replica_groups=mesh['prec'=16,'run'=2] {'prec'}, use_global_device_ids=true, to_apply=%region_0.0 | all-reduce | flops 4096 | bytes 32768 | tf_op jit(solution)/shard_map/psum | solution.py:41
  83.7 5.8 cholesky.134
  89.6 0.7 compare_reduce_fusion.7
  90.9 4.9 custom-call.18
  95.8 1.0 fusion.30
  97.3 17.5 %all_gather.12 = bf16[512,64]{1,0:T(8,128)(2,1)S(1)} all-gather(bf16[32,64]{1,0:T(8,128)(2,1)S(1)} %fusion.31), channel_id=1, replica_groups=mesh['prec'=16,'run'=2] {'prec'}, dimensions={0}, use_global_device_ids=true | all-gather | bytes 69632 | tf_op jit(solution)/shard_map/all_gather | solution.py:48
  115.0 4.3 convolution_convert_fusion.7
  119.3 8.2 %psum.85 = bf16[64,64]{0,1:T(8,128)(2,1)S(1)} all-reduce(bf16[64,64]{0,1:T(8,128)(2,1)S(1)} %convolution_convert_fusion.11), channel_id=1, replica_groups=mesh['prec'=16,'run'=2] {'run'}, use_global_device_ids=true, to_apply=%region_4.7 | all-reduce | flops 4096 | bytes 16384 | tf_op jit(solution)/shard_map/psum | solution.py:56
  127.6 5.9 cholesky.145
  133.6 0.6 compare_reduce_fusion.6
  134.8 4.9 custom-call.19
  139.7 15.1 %all-reduce.5.cloned.1.call-done = bf16[2048,64]{0,1:T(8,128)(2,1)} async-done(((bf16[2048,64]{0,1:T(8,128)(2,1)}), bf16[2048,64]{0,1:T(8,128)(2,1)}) %all-reduce.5.cloned.1.call-update) | async-done | bytes 262160 | tf_op jit(solution)/shard_map/psum | solution.py:55
  154.8 1.2 fusion.22
  155.9 0.6 fusion.68
  157.4 4.3 fusion.25
  161.7 61.2 %psum.87 = f32[64,64]{0,1:T(8,128)S(1)} all-reduce(f32[64,64]{0,1:T(8,128)S(1)} %fusion.104), channel_id=1, replica_groups=mesh['prec'=16,'run'=2] {'prec'}, use_global_device_ids=true, to_apply=%region_6.0 | all-reduce | flops 4096 | bytes 32768 | tf_op jit(solution)/shard_map/psum | solution.py:41
  223.0 5.8 cholesky.156
  228.9 0.7 compare_reduce_fusion.5
  230.3 4.9 custom-call.20
  235.2 46.6 %reduce-scatter.7.cloned.1.call-done = f32[32,64]{1,0:T(8,128)} async-done(((f32[512,64]{1,0:T(8,128)}), f32[32,64]{1,0:T(8,128)}) %reduce-scatter.7.cloned.1.call-update) | async-done | bytes 8208 | tf_op jit(solution)/shard_map/reduce_scatter | solution.py:42
  281.8 0.8 fusion.29
  283.2 19.8 %all_gather.13 = bf16[512,64]{1,0:T(8,128)(2,1)S(1)} all-gather(bf16[32,64]{1,0:T(8,128)(2,1)S(1)} %fusion.32), channel_id=1, replica_groups=mesh['prec'=16,'run'=2] {'prec'}, dimensions={0}, use_global_device_ids=true | all-gather | bytes 69632 | tf_op jit(solution)/shard_map/all_gather | solution.py:48
  303.2 4.6 convolution_convert_fusion.2
  307.7 8.1 %psum.88 = bf16[64,64]{0,1:T(8,128)(2,1)S(1)} all-reduce(bf16[64,64]{0,1:T(8,128)(2,1)S(1)} %convolution_convert_fusion.10), channel_id=1, replica_groups=mesh['prec'=16,'run'=2] {'run'}, use_global_device_ids=true, to_apply=%region_8.0 | all-reduce | flops 4096 | bytes 16384 | tf_op jit(solution)/shard_map/psum | solution.py:56
  316.0 5.8 cholesky.167
  323.1 4.9 custom-call.21
  328.0 19.0 %all-reduce.7.cloned.1.call-done = bf16[2048,64]{1,0:T(8,128)(2,1)} async-done(((bf16[2048,64]{1,0:T(8,128)(2,1)}), bf16[2048,64]{1,0:T(8,128)(2,1)}) %all-reduce.7.cloned.1.call-update) | async-done | bytes 262160 | tf_op jit(solution)/shard_map/psum | solution.py:55
  347.0 1.4 fusion.20
  348.4 1.3 fusion.60
  350.5 4.3 fusion.24
  354.8 61.0 %psum.90 = f32[64,64]{0,1:T(8,128)S(1)} all-reduce(f32[64,64]{0,1:T(8,128)S(1)} %fusion.105), channel_id=1, replica_groups=mesh['prec'=16,'run'=2] {'prec'}, use_global_device_ids=true, to_apply=%region_10.0 | all-reduce | flops 4096 | bytes 32768 | tf_op jit(solution)/shard_map/psum | solution.py:41
  415.9 5.8 cholesky.178
  421.8 0.7 compare_reduce_fusion.3
  423.2 4.9 custom-call.22
  428.1 46.6 %reduce-scatter.9.cloned.1.call-done = f32[32,64]{1,0:T(8,128)} async-done(((f32[512,64]{1,0:T(8,128)}), f32[32,64]{1,0:T(8,128)}) %reduce-scatter.9.cloned.1.call-update) | async-done | bytes 8208 | tf_op jit(solution)/shard_map/reduce_scatter | solution.py:42
  474.7 0.8 fusion.28
  476.1 19.9 %all_gather.14 = bf16[512,64]{1,0:T(8,128)(2,1)S(1)} all-gather(bf16[32,64]{1,0:T(8,128)(2,1)S(1)} %fusion.33), channel_id=1, replica_groups=mesh['prec'=16,'run'=2] {'prec'}, dimensions={0}, use_global_device_ids=true | all-gather | bytes 69632 | tf_op jit(solution)/shard_map/all_gather | solution.py:48
  496.2 4.6 convolution_convert_fusion.1
  500.8 8.1 %psum.91 = bf16[64,64]{0,1:T(8,128)(2,1)S(1)} all-reduce(bf16[64,64]{0,1:T(8,128)(2,1)S(1)} %convolution_convert_fusion.9), channel_id=1, replica_groups=mesh['prec'=16,'run'=2] {'run'}, use_global_device_ids=true, to_apply=%region_12.0 | all-reduce | flops 4096 | bytes 16384 | tf_op jit(solution)/shard_map/psum | solution.py:56
  509.0 5.8 cholesky.189
  516.1 4.9 custom-call.23
  521.0 19.0 %all-reduce.9.cloned.1.call-done = bf16[2048,64]{1,0:T(8,128)(2,1)} async-done(((bf16[2048,64]{1,0:T(8,128)(2,1)}), bf16[2048,64]{1,0:T(8,128)(2,1)}) %all-reduce.9.cloned.1.call-update) | async-done | bytes 262160 | tf_op jit(solution)/shard_map/psum | solution.py:55
  540.1 1.4 fusion.19
  541.5 1.3 fusion.52
  543.5 4.3 fusion.23
  547.9 61.0 %psum.93 = f32[64,64]{0,1:T(8,128)S(1)} all-reduce(f32[64,64]{0,1:T(8,128)S(1)} %fusion.106), channel_id=1, replica_groups=mesh['prec'=16,'run'=2] {'prec'}, use_global_device_ids=true, to_apply=%region_14.0 | all-reduce | flops 4096 | bytes 32768 | tf_op jit(solution)/shard_map/psum | solution.py:41
  609.0 5.8 cholesky.200
  614.9 0.7 compare_reduce_fusion.1
  616.2 4.9 custom-call.24
  621.1 46.6 %reduce-scatter.11.cloned.1.call-done = f32[32,64]{1,0:T(8,128)} async-done(((f32[512,64]{1,0:T(8,128)}), f32[32,64]{1,0:T(8,128)}) %reduce-scatter.11.cloned.1.call-update) | async-done | bytes 8208 | tf_op jit(solution)/shard_map/reduce_scatter | solution.py:42
  667.8 0.8 fusion.27
  669.1 19.8 %all_gather.15 = bf16[512,64]{1,0:T(8,128)(2,1)S(1)} all-gather(bf16[32,64]{1,0:T(8,128)(2,1)S(1)} %fusion.34), channel_id=1, replica_groups=mesh['prec'=16,'run'=2] {'prec'}, dimensions={0}, use_global_device_ids=true | all-gather | bytes 69632 | tf_op jit(solution)/shard_map/all_gather | solution.py:48
  689.1 4.6 convolution_convert_fusion
  693.7 8.3 %psum.94 = bf16[64,64]{0,1:T(8,128)(2,1)S(1)} all-reduce(bf16[64,64]{0,1:T(8,128)(2,1)S(1)} %convolution_convert_fusion.8), channel_id=1, replica_groups=mesh['prec'=16,'run'=2] {'run'}, use_global_device_ids=true, to_apply=%region_16.20 | all-reduce | flops 4096 | bytes 16384 | tf_op jit(solution)/shard_map/psum | solution.py:56
  702.1 5.8 cholesky.211
  709.2 4.9 custom-call.25
  714.1 19.1 %all-reduce.11.cloned.1.call-done = bf16[2048,64]{1,0:T(8,128)(2,1)} async-done(((bf16[2048,64]{1,0:T(8,128)(2,1)}), bf16[2048,64]{1,0:T(8,128)(2,1)}) %all-reduce.11.cloned.1.call-update) | async-done | bytes 262160 | tf_op jit(solution)/shard_map/psum | solution.py:55
  733.2 1.5 fusion.18
  734.7 1.3 fusion.44
  736.6 2.7 fusion.1
  (90 shorter events, 14.1 us)
Async XLA Ops:
  6.5 9.4 %copy-start = (bf16[2048,64]{0,1:T(8,128)(2,1)S(1)}, bf16[2048,64]{0,1:T(8,128)(2,1)}, u32[]{:S(2)}) copy-start(bf16[2048,64]{0,1:T(8,128)(2,1)} %param.12) | copy-start | bytes 786436
  6.5 89.3 %reduce-scatter.5.cloned.1.call-start = ((), (), s32[]{:S(2)}) async-start(), calls=%async_computation.4 | async-start | bytes 278528 | tf_op jit(solution)/shard_map/reduce_scatter | solution.py:42
  10.3 5.7 copy-start.2
  10.3 5.7 copy-start.3
  20.4 134.4 %all-reduce.5.cloned.1.call-start = ((), (), s32[]{:S(2)}) async-start(), calls=%async_computation.5 | async-start | bytes 524288 | tf_op jit(solution)/shard_map/psum | solution.py:55
  133.5 148.3 %reduce-scatter.7.cloned.1.call-start = ((), (), s32[]{:S(2)}) async-start(), calls=%async_computation.6 | async-start | bytes 278528 | tf_op jit(solution)/shard_map/reduce_scatter | solution.py:42
  229.6 117.4 %all-reduce.7.cloned.1.call-start = ((), (), s32[]{:S(2)}) async-start(), calls=%async_computation.7 | async-start | bytes 1048576 | tf_op jit(solution)/shard_map/psum | solution.py:55
  321.9 152.8 %reduce-scatter.9.cloned.1.call-start = ((), (), s32[]{:S(2)}) async-start(), calls=%async_computation.8 | async-start | bytes 278528 | tf_op jit(solution)/shard_map/reduce_scatter | solution.py:42
  422.5 117.6 %all-reduce.9.cloned.1.call-start = ((), (), s32[]{:S(2)}) async-start(), calls=%async_computation.9 | async-start | bytes 1048576 | tf_op jit(solution)/shard_map/psum | solution.py:55
  514.9 152.8 %reduce-scatter.11.cloned.1.call-start = ((), (), s32[]{:S(2)}) async-start(), calls=%async_computation.10 | async-start | bytes 278528 | tf_op jit(solution)/shard_map/reduce_scatter | solution.py:42
  615.6 117.6 %all-reduce.11.cloned.1.call-start = ((), (), s32[]{:S(2)}) async-start(), calls=%async_computation.11 | async-start | bytes 1048576 | tf_op jit(solution)/shard_map/psum | solution.py:55
  733.2 3.4 copy-start.1
Sparse Core Ops, SparseCore 0:
  20.5 58.5 reduce-scatter.4
  133.6 21.0 all-reduce.4
  229.7 52.0 reduce-scatter.6
  322.0 24.9 all-reduce.6
  422.6 52.0 reduce-scatter.8
  515.0 24.9 all-reduce.8
  615.7 52.0 reduce-scatter.10
  708.2 24.9 all-reduce.10
where the time goes:
time: 755 us; the launch traced here: 746 us
  blocking collectives  356 us (47%)
  waiting for transfers between devices  212 us (28%)
  other arithmetic  96.2 us (13%)
  matrix products  57.4 us (8%)
  between operations  14.2 us (2%)
  local copies, waits for them, and re-layouts  10 us (1%)
    psum x4, blocking collectives, local(): gram_v = lax.psum(gram_part, 'prec')  246 us
    reduce_scatter x4, waiting for transfers between devices, local(): share = lax.psum_scatter(proj_part, 'prec', scatter_dimension=0, tiled=True)  140 us
    all_gather x4, blocking collectives, local(): u_now = lax.all_gather(fresh, 'prec', axis=0, tiled=True)  77 us
    psum x4, waiting for transfers between devices, local(): lax.psum(proj_part.astype(jnp.bfloat16), 'run').astype(jnp.float32)  72.2 us
    another operation x24, other arithmetic, ridge_solve(): jnp.linalg.cholesky(gram + ridge_value * jnp.eye(size, dtype=jnp.float32))  52.2 us
    another operation x16, other arithmetic, ridge_solve(): return jax.scipy.linalg.cho_solve((factor, True), matrix.T).T  43.9 us
    psum x4, blocking collectives, local(): lax.psum(gram_part.astype(jnp.bfloat16), 'run').astype(jnp.float32)  32.7 us
    dot_general x4, matrix products, local(): lax.dot_general(resid, u_now, (((0,), (0,)), ((), ())), preferred_element...  18.1 us
  transfers between devices with their start and end apart: 8, of which 7 were waited for; matrix products, arithmetic and copies ran while one was open for 7% of the time, Pallas kernels for 0%

commit v1 on v0

--- a/solution.py
+++ b/solution.py
@@ -1,3 +1,4 @@
+import functools
 import jax
 import jax.numpy as jnp
 from jax import lax
@@ -5,6 +6,13 @@
 
 ITERS = 4
 ridge_value = 16.0
+
+
+def _post_pairs_all(own_rows, dev_axis):
+    return jnp.sum(lax.all_gather(own_rows, axis_name=dev_axis), axis=0)
+
+
+drive_core_all = functools.partial(_post_pairs_all, dev_axis="prec")
 
 
 def unpack_mask(words):
@@ -38,7 +46,7 @@
         resid = masked_resid(intensity, maskf, u_now, v_now)
         proj_part = jnp.dot(resid, v_now, preferred_element_type=jnp.float32)
         gram_part = inner_gram(v_now)
-        gram_v = lax.psum(gram_part, "prec")
+        gram_v = drive_core_all(gram_part)
         share = lax.psum_scatter(proj_part, "prec", scatter_dimension=0, tiled=True)
         count = share.shape[0]
         first = lax.axis_index("prec") * count

time: 755 us -> 607 us (0.80)
  blocking collectives: 356 us -> 206 us
    psum x4 -> x0, blocking collectives: 246 us -> none  [local(): gram_v = lax.psum(gram_part, 'prec')]
    all_gather x0 -> x4, blocking collectives: none -> 93.7 us  [_post_pairs_all(): return jnp.sum(lax.all_gather(own_rows, axis_name=dev_axis), axis=0)]
    reduce_scatter x4, waiting for transfers between devices: 140 us -> 161 us  [local(): share = lax.psum_scatter(proj_part, 'prec', scatter_dimension=0, tiled=True)]
    psum x4, waiting for transfers between devices: 72.2 us -> 54.4 us  [local(): lax.psum(proj_part.astype(jnp.bfloat16), 'run').astype(jnp.float32)]
  transfers between devices with their start and end apart: 8 -> 8, of which waited for: 7 -> 8; matrix products, arithmetic and copies ran while one was open for 7% -> 9% of each run, Pallas kernels for 0% -> 0%
where the time goes in v1:
time: 607 us; the launch traced here: 598 us
  waiting for transfers between devices  216 us (36%)
  blocking collectives  206 us (34%)
  other arithmetic  96.6 us (16%)
  matrix products  55.3 us (9%)
  between operations  14.2 us (2%)
  local copies, waits for them, and re-layouts  10.3 us (2%)
    reduce_scatter x4, waiting for transfers between devices, local(): share = lax.psum_scatter(proj_part, 'prec', scatter_dimension=0, tiled=True)  161 us
    all_gather x4, blocking collectives, _post_pairs_all(): return jnp.sum(lax.all_gather(own_rows, axis_name=dev_axis), axis=0)  93.7 us
    all_gather x4, blocking collectives, local(): u_now = lax.all_gather(fresh, 'prec', axis=0, tiled=True)  79.3 us
    psum x4, waiting for transfers between devices, local(): lax.psum(proj_part.astype(jnp.bfloat16), 'run').astype(jnp.float32)  54.4 us
    another operation x24, other arithmetic, ridge_solve(): jnp.linalg.cholesky(gram + ridge_value * jnp.eye(size, dtype=jnp.float32))  52.3 us
    another operation x16, other arithmetic, ridge_solve(): return jax.scipy.linalg.cho_solve((factor, True), matrix.T).T  43.9 us
    psum x4, blocking collectives, local(): lax.psum(gram_part.astype(jnp.bfloat16), 'run').astype(jnp.float32)  32.7 us
    dot_general x4, matrix products, local(): proj_part = jnp.dot(resid, v_now, preferred_element_type=jnp.float32)  17.3 us
  transfers between devices with their start and end apart: 8, of which 8 were waited for; matrix products, arithmetic and copies ran while one was open for 9% of the time, Pallas kernels for 0%

profile of v1, /device:TPU:0, one launch (start us, length us, event | category | flops | bytes accessed | tf_op | source)
XLA Modules:
  0.0 598.5 jit_solution(11315393526274863771)
XLA Ops:
  6.5 1.3 copy.31
  7.8 2.5 broadcast_bitcast_fusion
  10.3 5.5 copy.32
  16.0 4.4 fusion.26
  20.7 24.6 %all-gather = f32[1024,64]{1,0:T(8,128)S(1)} all-gather(f32[64,64]{1,0:T(8,128)S(1)} %fusion.103), channel_id=2, replica_groups=mesh['prec'=16,'run'=2] {'prec'}, dimensions={0}, use_global_device_ids=true | all-gather | bytes 278528 | tf_op jit(solution)/shard_map/all_gather | solution.py:12
  45.5 5.8 cholesky.134
  51.4 0.7 compare_reduce_fusion.7
  52.7 4.9 custom-call.18
  57.6 21.6 %reduce-scatter.5.cloned.1.call-done = f32[32,64]{1,0:T(8,128)} async-done(((f32[512,64]{1,0:T(8,128)}), f32[32,64]{1,0:T(8,128)}) %reduce-scatter.5.cloned.1.call-update) | async-done | bytes 8208 | tf_op jit(solution)/shard_map/reduce_scatter | solution.py:50
  79.1 1.0 fusion.30
  80.5 19.8 %all_gather.38 = bf16[512,64]{1,0:T(8,128)(2,1)S(1)} all-gather(bf16[32,64]{1,0:T(8,128)(2,1)S(1)} %fusion.31), channel_id=1, replica_groups=mesh['prec'=16,'run'=2] {'prec'}, dimensions={0}, use_global_device_ids=true | all-gather | bytes 69632 | tf_op jit(solution)/shard_map/all_gather | solution.py:56
  100.5 4.3 convolution_convert_fusion.7
  104.8 8.1 %psum.56 = bf16[64,64]{0,1:T(8,128)(2,1)S(1)} all-reduce(bf16[64,64]{0,1:T(8,128)(2,1)S(1)} %convolution_convert_fusion.11), channel_id=1, replica_groups=mesh['prec'=16,'run'=2] {'run'}, use_global_device_ids=true, to_apply=%region_4.7 | all-reduce | flops 4096 | bytes 16384 | tf_op jit(solution)/shard_map/psum | solution.py:64
  113.0 5.8 cholesky.145
  119.0 0.6 compare_reduce_fusion.6
  120.2 4.9 custom-call.19
  125.1 13.6 %all-reduce.5.cloned.1.call-done = bf16[2048,64]{0,1:T(8,128)(2,1)} async-done(((bf16[2048,64]{0,1:T(8,128)(2,1)}), bf16[2048,64]{0,1:T(8,128)(2,1)}) %all-reduce.5.cloned.1.call-update) | async-done | bytes 262160 | tf_op jit(solution)/shard_map/psum | solution.py:63
  138.7 1.2 fusion.22
  141.3 4.3 fusion.25
  145.6 23.3 %all-gather.1 = f32[1024,64]{1,0:T(8,128)S(1)} all-gather(f32[64,64]{1,0:T(8,128)S(1)} %fusion.104), channel_id=3, replica_groups=mesh['prec'=16,'run'=2] {'prec'}, dimensions={0}, use_global_device_ids=true | all-gather | bytes 278528 | tf_op jit(solution)/shard_map/all_gather | solution.py:12
  169.2 5.9 cholesky.156
  175.1 0.7 compare_reduce_fusion.5
  176.4 4.9 custom-call.20
  181.3 46.6 %reduce-scatter.7.cloned.1.call-done = f32[32,64]{1,0:T(8,128)} async-done(((f32[512,64]{1,0:T(8,128)}), f32[32,64]{1,0:T(8,128)}) %reduce-scatter.7.cloned.1.call-update) | async-done | bytes 8208 | tf_op jit(solution)/shard_map/reduce_scatter | solution.py:50
  228.0 0.8 fusion.29
  229.2 19.8 %all_gather.41 = bf16[512,64]{1,0:T(8,128)(2,1)S(1)} all-gather(bf16[32,64]{1,0:T(8,128)(2,1)S(1)} %fusion.32), channel_id=1, replica_groups=mesh['prec'=16,'run'=2] {'prec'}, dimensions={0}, use_global_device_ids=true | all-gather | bytes 69632 | tf_op jit(solution)/shard_map/all_gather | solution.py:56
  249.2 4.3 convolution_convert_fusion.5
  253.5 8.1 %psum.58 = bf16[64,64]{0,1:T(8,128)(2,1)S(1)} all-reduce(bf16[64,64]{0,1:T(8,128)(2,1)S(1)} %convolution_convert_fusion.10), channel_id=1, replica_groups=mesh['prec'=16,'run'=2] {'run'}, use_global_device_ids=true, to_apply=%region_8.0 | all-reduce | flops 4096 | bytes 16384 | tf_op jit(solution)/shard_map/psum | solution.py:64
  261.7 5.8 cholesky.167
  267.7 0.6 compare_reduce_fusion.4
  268.9 4.9 custom-call.21
  273.8 13.6 %all-reduce.7.cloned.1.call-done = bf16[2048,64]{0,1:T(8,128)(2,1)} async-done(((bf16[2048,64]{0,1:T(8,128)(2,1)}), bf16[2048,64]{0,1:T(8,128)(2,1)}) %all-reduce.7.cloned.1.call-update) | async-done | bytes 262160 | tf_op jit(solution)/shard_map/psum | solution.py:63
  287.4 1.2 fusion.18
  290.0 4.3 fusion.24
  294.3 22.9 %all-gather.2 = f32[1024,64]{1,0:T(8,128)S(1)} all-gather(f32[64,64]{1,0:T(8,128)S(1)} %fusion.105), channel_id=4, replica_groups=mesh['prec'=16,'run'=2] {'prec'}, dimensions={0}, use_global_device_ids=true | all-gather | bytes 278528 | tf_op jit(solution)/shard_map/all_gather | solution.py:12
  317.4 5.9 cholesky.178
  323.3 0.7 compare_reduce_fusion.3
  324.7 4.9 custom-call.22
  329.6 46.6 %reduce-scatter.9.cloned.1.call-done = f32[32,64]{1,0:T(8,128)} async-done(((f32[512,64]{1,0:T(8,128)}), f32[32,64]{1,0:T(8,128)}) %reduce-scatter.9.cloned.1.call-update) | async-done | bytes 8208 | tf_op jit(solution)/shard_map/reduce_scatter | solution.py:50
  376.2 0.8 fusion.28
  377.4 19.9 %all_gather.44 = bf16[512,64]{1,0:T(8,128)(2,1)S(1)} all-gather(bf16[32,64]{1,0:T(8,128)(2,1)S(1)} %fusion.33), channel_id=1, replica_groups=mesh['prec'=16,'run'=2] {'prec'}, dimensions={0}, use_global_device_ids=true | all-gather | bytes 69632 | tf_op jit(solution)/shard_map/all_gather | solution.py:56
  397.6 4.3 convolution_convert_fusion.3
  401.9 8.1 %psum.60 = bf16[64,64]{0,1:T(8,128)(2,1)S(1)} all-reduce(bf16[64,64]{0,1:T(8,128)(2,1)S(1)} %convolution_convert_fusion.9), channel_id=1, replica_groups=mesh['prec'=16,'run'=2] {'run'}, use_global_device_ids=true, to_apply=%region_12.0 | all-reduce | flops 4096 | bytes 16384 | tf_op jit(solution)/shard_map/psum | solution.py:64
  410.1 5.8 cholesky.189
  416.1 0.6 compare_reduce_fusion.2
  417.3 4.9 custom-call.23
  422.2 13.6 %all-reduce.9.cloned.1.call-done = bf16[2048,64]{0,1:T(8,128)(2,1)} async-done(((bf16[2048,64]{0,1:T(8,128)(2,1)}), bf16[2048,64]{0,1:T(8,128)(2,1)}) %all-reduce.9.cloned.1.call-update) | async-done | bytes 262160 | tf_op jit(solution)/shard_map/psum | solution.py:63
  435.8 1.2 fusion.19
  438.4 4.3 fusion.23
  442.7 22.9 %all-gather.3 = f32[1024,64]{1,0:T(8,128)S(1)} all-gather(f32[64,64]{1,0:T(8,128)S(1)} %fusion.106), channel_id=5, replica_groups=mesh['prec'=16,'run'=2] {'prec'}, dimensions={0}, use_global_device_ids=true | all-gather | bytes 278528 | tf_op jit(solution)/shard_map/all_gather | solution.py:12
  465.8 5.9 cholesky.200
  471.7 0.7 compare_reduce_fusion.1
  473.1 4.9 custom-call.24
  478.0 46.6 %reduce-scatter.11.cloned.1.call-done = f32[32,64]{1,0:T(8,128)} async-done(((f32[512,64]{1,0:T(8,128)}), f32[32,64]{1,0:T(8,128)}) %reduce-scatter.11.cloned.1.call-update) | async-done | bytes 8208 | tf_op jit(solution)/shard_map/reduce_scatter | solution.py:50
  524.6 0.8 fusion.27
  525.8 19.8 %all_gather.47 = bf16[512,64]{1,0:T(8,128)(2,1)S(1)} all-gather(bf16[32,64]{1,0:T(8,128)(2,1)S(1)} %fusion.34), channel_id=1, replica_groups=mesh['prec'=16,'run'=2] {'prec'}, dimensions={0}, use_global_device_ids=true | all-gather | bytes 69632 | tf_op jit(solution)/shard_map/all_gather | solution.py:56
  545.8 4.3 convolution_convert_fusion.1
  550.1 8.3 %psum.62 = bf16[64,64]{0,1:T(8,128)(2,1)S(1)} all-reduce(bf16[64,64]{0,1:T(8,128)(2,1)S(1)} %convolution_convert_fusion.8), channel_id=1, replica_groups=mesh['prec'=16,'run'=2] {'run'}, use_global_device_ids=true, to_apply=%region_16.20 | all-reduce | flops 4096 | bytes 16384 | tf_op jit(solution)/shard_map/psum | solution.py:64
  558.6 5.8 cholesky.211
  564.5 0.6 compare_reduce_fusion
  565.7 4.9 custom-call.25
  570.6 13.6 %all-reduce.11.cloned.1.call-done = bf16[2048,64]{0,1:T(8,128)(2,1)} async-done(((bf16[2048,64]{0,1:T(8,128)(2,1)}), bf16[2048,64]{0,1:T(8,128)(2,1)}) %all-reduce.11.cloned.1.call-update) | async-done | bytes 262160 | tf_op jit(solution)/shard_map/psum | solution.py:63
  584.2 1.2 fusion.20
  586.6 4.8 fusion.1
  (96 shorter events, 14.7 us)
Async XLA Ops:
  6.5 9.4 %copy-start = (bf16[2048,64]{0,1:T(8,128)(2,1)S(1)}, bf16[2048,64]{0,1:T(8,128)(2,1)}, u32[]{:S(2)}) copy-start(bf16[2048,64]{0,1:T(8,128)(2,1)} %param.12) | copy-start | bytes 786436
  6.5 72.6 %reduce-scatter.5.cloned.1.call-start = ((), (), s32[]{:S(2)}) async-start(), calls=%async_computation.4 | async-start | bytes 278528 | tf_op jit(solution)/shard_map/reduce_scatter | solution.py:50
  10.3 5.7 copy-start.1
  10.3 5.7 copy-start.2
  20.4 118.3 %all-reduce.5.cloned.1.call-start = ((), (), s32[]{:S(2)}) async-start(), calls=%async_computation.5 | async-start | bytes 524288 | tf_op jit(solution)/shard_map/psum | solution.py:63
  118.9 109.1 %reduce-scatter.7.cloned.1.call-start = ((), (), s32[]{:S(2)}) async-start(), calls=%async_computation.6 | async-start | bytes 278528 | tf_op jit(solution)/shard_map/reduce_scatter | solution.py:50
  175.8 111.6 %all-reduce.7.cloned.1.call-start = ((), (), s32[]{:S(2)}) async-start(), calls=%async_computation.7 | async-start | bytes 524288 | tf_op jit(solution)/shard_map/psum | solution.py:63
  267.6 108.6 %reduce-scatter.9.cloned.1.call-start = ((), (), s32[]{:S(2)}) async-start(), calls=%async_computation.8 | async-start | bytes 278528 | tf_op jit(solution)/shard_map/reduce_scatter | solution.py:50
  324.0 111.8 %all-reduce.9.cloned.1.call-start = ((), (), s32[]{:S(2)}) async-start(), calls=%async_computation.9 | async-start | bytes 524288 | tf_op jit(solution)/shard_map/psum | solution.py:63
  416.0 108.6 %reduce-scatter.11.cloned.1.call-start = ((), (), s32[]{:S(2)}) async-start(), calls=%async_computation.10 | async-start | bytes 278528 | tf_op jit(solution)/shard_map/reduce_scatter | solution.py:50
  472.4 111.8 %all-reduce.11.cloned.1.call-start = ((), (), s32[]{:S(2)}) async-start(), calls=%async_computation.11 | async-start | bytes 524288 | tf_op jit(solution)/shard_map/psum | solution.py:63
Sparse Core Ops, SparseCore 0:
  20.5 58.5 reduce-scatter.4
  119.0 19.6 all-reduce.4
  175.9 52.0 reduce-scatter.6
  267.8 19.5 all-reduce.6
  324.1 52.0 reduce-scatter.8
  416.2 19.5 all-reduce.8
  472.5 52.0 reduce-scatter.10
  564.6 19.5 all-reduce.10
